TPU v7x, 32 devices: a whole 2x2x4 slice. The times are simulated.
32 devices in a mesh: groups: 2 (over y), blk: 4 (over z), cols: 2 (over x), sub: 2 (over core).
Axes of the slice: x: 2, y: 2, z: 4, core: 2. Of those that a mesh axis runs over, the one named last changes fastest.
Arguments:
- features: bfloat16 [4096, 256], P(('groups', 'blk', 'cols'), 'sub'), parts along dimension 0, may hold values from -60 to 60, as said below
- vector: float32 [4096], P(('groups', 'blk', 'cols')), parts along dimension 0, may hold values from 0.1 to 100, as said below
Outputs:
- new_vector: float32 [4096], P(('groups', 'blk', 'cols')), parts along dimension 0
- mean_affinity: float32 [4096], P(('groups', 'blk', 'cols')), parts along dimension 0
There are 2 independent parts, one for each index of `groups`. A program takes and returns all parts, laid end to end along the dimension named above; each array names one. Nothing has to cross between parts.
Inputs may be any that keep to these rules, and one draw needn't show every extreme that they name: Real-valued features; no row is zero. `vector`: positive entries.
All inputs are finite; a program needn't handle non-finite values. Where the computation divides by a largest or mean magnitude, that divisor is 1e-20 or more.
Results may differ from a plain program's by a relative error of at most 0.0033.
Values may be sent and summed in bfloat16 or wider, within the bound.
A program may use at most 64 MiB of HBM per device.

v0:
```python
import math
import jax
import jax.numpy as jnp
from jax import lax
from jax.sharding import PartitionSpec as P

POWER = 16


def fold_block(row_feats, totals, col_feats, col_vals):
    cosine = lax.dot_general(
        row_feats, col_feats, (((1,), (1,)), ((), ())), preferred_element_type=jnp.float32
    )
    affinity = (1.0 + cosine) * 0.5
    for level in range(POWER.bit_length() - 1):
        affinity = affinity * affinity
    weighted = totals[0] + jnp.dot(affinity, col_vals, precision=lax.Precision.HIGHEST)
    degree = totals[1] + jnp.sum(affinity, axis=1)
    return (weighted, degree)


def sweep(row_feats, totals, pieces):
    col_feats, col_vals = pieces
    columns = col_feats.shape[0]
    block_len = math.gcd(columns, 512)
    blocks = columns // block_len
    if blocks == 1:
        return fold_block(row_feats, totals, col_feats, col_vals)
    stacked = (
        col_feats.reshape(blocks, block_len, col_feats.shape[1]),
        col_vals.reshape(blocks, block_len),
    )

    def advance(running, member):
        return (fold_block(row_feats, running, member[0], member[1]), None)

    result, unused = lax.scan(advance, totals, stacked)
    return result


def empty_sums(length):
    return (jnp.zeros((length,), jnp.float32), jnp.zeros((length,), jnp.float32))


def local(features, vector):
    own_rows = features.shape[0]
    half_rows = own_rows // 2
    gathered = lax.all_gather(features, "sub", axis=1, tiled=True)
    widened = gathered.astype(jnp.float32)
    unit_rows = (
        widened
        * lax.rsqrt(jnp.mean(widened * widened, axis=1, keepdims=True) + 1e-06)
        * (1.0 / math.sqrt(widened.shape[1]))
    ).astype(jnp.bfloat16)
    sub_index = lax.axis_index("sub")
    col_feats = lax.dynamic_slice_in_dim(unit_rows, sub_index * half_rows, half_rows, 0)
    col_vals = lax.dynamic_slice_in_dim(vector, sub_index * half_rows, half_rows, 0)
    points = own_rows * lax.axis_size("blk") * lax.axis_size("cols")
    block_feats = lax.all_gather(unit_rows, "cols", axis=0, tiled=True)
    partial_sums = sweep(
        block_feats,
        empty_sums(block_feats.shape[0]),
        (
            lax.all_gather(col_feats, "blk", axis=0, tiled=True),
            lax.all_gather(col_vals.astype(jnp.bfloat16), "blk", axis=0, tiled=True).astype(
                jnp.float32
            ),
        ),
    )
    block_weighted, block_degree = lax.psum((partial_sums[0], partial_sums[1]), ("cols", "sub"))
    block_averaged = block_weighted / block_degree
    total = lax.psum(jnp.sum(jnp.abs(block_averaged)), "blk")
    first_row = lax.axis_index("cols") * own_rows
    averaged = lax.dynamic_slice_in_dim(block_averaged, first_row, own_rows, 0)
    degree = lax.dynamic_slice_in_dim(block_degree, first_row, own_rows, 0)
    mean_abs = total / points + 1e-06
    return (averaged / mean_abs, degree / points)


def solution(mesh):
    in_specs = (P(("groups", "blk", "cols"), "sub"), P(("groups", "blk", "cols")))
    out_specs = (P(("groups", "blk", "cols")), P(("groups", "blk", "cols")))
    return jax.shard_map(local, mesh=mesh, in_specs=in_specs, out_specs=out_specs, check_vma=False)
```

profile of v0, /device:TPU:0, one launch (start us, length us, event | category | flops | bytes accessed | tf_op | source)
XLA Modules:
  0.0 53.8 jit_solution(12219842867503228828)
XLA Ops:
  0.6 0.0 copy-start
  0.7 2.3 %all_gather.12 = bf16[256,256]{1,0:T(8,128)(2,1)S(1)} all-gather(bf16[256,128]{1,0:T(8,128)(2,1)} %param.2), channel_id=1, replica_groups=mesh['groups'=2,'blk'=4,'cols'=2,'sub'=2] {'sub'}, dimensions={1}, use_global_device_ids=true | all-gather | bytes 196608 | tf_op jit(solution)/shard_map/all_gather | solution.py:48
  2.9 0.1 fusion.5
  3.1 0.1 fusion.7
  3.2 15.4 %all_gather.14 = bf16[512,256]{1,0:T(8,128)(2,1)S(1)} all-gather(bf16[128,256]{1,0:T(8,128)(2,1)S(1)} %constant_dynamic-slice_fusion), channel_id=1, replica_groups=mesh['groups'=2,'blk'=4,'cols'=2,'sub'=2] {'blk'}, dimensions={0}, use_global_device_ids=true | all-gather | bytes 327680 | tf_op jit(solution)/shard_map/all_gather | solution.py:64
  18.6 5.6 %all_gather.13 = bf16[512,256]{1,0:T(8,128)(2,1)S(1)} all-gather(bf16[256,256]{1,0:T(8,128)(2,1)S(1)} %fusion.7), channel_id=1, replica_groups=mesh['groups'=2,'blk'=4,'cols'=2,'sub'=2] {'cols'}, dimensions={0}, use_global_device_ids=true | all-gather | bytes 393216 | tf_op jit(solution)/shard_map/all_gather | solution.py:59
  24.2 0.4 fusion.10
  24.6 0.0 copy-done
  24.6 0.1 convert_bitcast_fusion
  24.7 11.5 %all-gather = bf16[4,1,128]{2,1,0:T(2,128)(2,1)S(1)} all-gather(bf16[1,1,128]{2,1,0:T(2,128)(2,1)S(1)} %convert_bitcast_fusion), channel_id=1, replica_groups=mesh['groups'=2,'blk'=4,'cols'=2,'sub'=2] {'blk'}, dimensions={0}, use_global_device_ids=true | all-gather | bytes 1280 | tf_op jit(solution)/shard_map/all_gather | solution.py:65
  36.2 0.4 fusion.8
  36.7 5.6 %all-reduce = (f32[512]{0:T(512)S(1)}, f32[512]{0:T(512)S(1)}) all-reduce(f32[512]{0:T(512)S(1)} %bitcast.9, f32[512]{0:T(512)S(1)} %get-tuple-element.6), channel_id=1, replica_groups=mesh['groups'=2,'blk'=4,'cols'=2,'sub'=2] {'cols','sub'}, use_global_device_ids=true, to_apply=%region_1.0 | all-reduce | flops 1024 | bytes 8192 | tf_op jit(solution)/shard_map/psum | solution.py:70
  42.3 0.6 %dynamic-slice_multiply_fusion = f32[256]{0:T(256)} fusion(f32[512]{0:T(512)S(1)} %get-tuple-element.3, s32[]{:T(128)S(6)} %select_n.9), kind=kLoop, calls=%fused_computation.14 | loop fusion | flops 256 | bytes 2052 | tf_op jit(solution)/shard_map/div | solution.py:77
  43.0 0.6 %abs_reduce_fusion = (f32[]{:T(128)}, f32[512]{0:T(512)S(1)}) fusion(f32[512]{0:T(512)S(1)} %get-tuple-element.2, f32[512]{0:T(512)S(1)} %get-tuple-element.3), kind=kLoop, calls=%fused_computation.13 | loop fusion | flops 1535 | bytes 6148 | tf_op jit(solution)/shard_map/reduce_sum | solution.py:72
  43.6 9.0 %psum.23 = f32[]{:T(128)} all-reduce(f32[]{:T(128)} %get-tuple-element.4), channel_id=1, replica_groups=mesh['groups'=2,'blk'=4,'cols'=2,'sub'=2] {'blk'}, use_global_device_ids=true, to_apply=%region_5.0 | all-reduce | flops 1 | bytes 8 | tf_op jit(solution)/shard_map/psum | solution.py:72
  53.2 0.6 %dynamic-slice_divide_fusion = f32[256]{0:T(256)} fusion(f32[512]{0:T(512)S(1)} %get-tuple-element.5, s32[]{:T(128)S(6)} %select_n.9, f32[]{:T(128)S(6)} %add.40), kind=kLoop, calls=%fused_computation.15 | loop fusion | flops 256 | bytes 2056 | tf_op jit(solution)/shard_map/div | solution.py:77
  (2 shorter events, 0.0 us)
Async XLA Ops:
  0.6 24.0 %copy-start = (f32[256]{0:T(256)S(1)}, f32[256]{0:T(256)}, u32[]{:S(2)}) copy-start(f32[256]{0:T(256)} %param.3) | copy-start | bytes 3076
where the time goes:
time: 54.1 us; the launch traced here: 53.8 us
  blocking collectives  49.4 us (91%)
  other arithmetic  2.11 us (4%)
  between operations  1.34 us (2%)
  matrix products  0.89 us (2%)
    all_gather x1, blocking collectives, local(): lax.all_gather(col_feats, 'blk', axis=0, tiled=True)  15.4 us
    all_gather x1, blocking collectives, local(): lax.all_gather(col_vals.astype(jnp.bfloat16), 'blk', axis=0, tiled=True)  11.5 us
    psum x1, blocking collectives, local(): total = lax.psum(jnp.sum(jnp.abs(block_averaged)), 'blk')  8.97 us
    psum x1, blocking collectives, local(): lax.psum((partial_sums[0], partial_sums[1]), ('cols', 'sub'))  5.64 us
    all_gather x1, blocking collectives, local(): block_feats = lax.all_gather(unit_rows, 'cols', axis=0, tiled=True)  5.62 us
    all_gather x1, blocking collectives, local(): gathered = lax.all_gather(features, 'sub', axis=1, tiled=True)  2.28 us
    div x2, other arithmetic, local(): return (averaged / mean_abs, degree / points)  1.28 us

commit v1 on v0

--- a/solution.py
+++ b/solution.py
@@ -67,7 +67,9 @@
             ),
         ),
     )
-    block_weighted, block_degree = lax.psum((partial_sums[0], partial_sums[1]), ("cols", "sub"))
+    block_weighted, block_degree = lax.psum(
+        lax.psum((partial_sums[0], partial_sums[1]), "sub"), "cols"
+    )
     block_averaged = block_weighted / block_degree
     total = lax.psum(jnp.sum(jnp.abs(block_averaged)), "blk")
     first_row = lax.axis_index("cols") * own_rows

time: 54.1 us -> 55.8 us (1.031)
  blocking collectives: 49.4 us -> 51.1 us
    psum x1 -> x2, blocking collectives: 5.64 us -> 7.36 us  [the longest x1 4.91 us: local(): lax.psum(lax.psum((partial_sums[0], partial_sums[1]), 'sub'), 'cols')]
where the time goes in v1:
time: 55.8 us; the launch traced here: 55.6 us
  blocking collectives  51.1 us (92%)
  other arithmetic  2.11 us (4%)
  between operations  1.34 us (2%)
  matrix products  0.89 us (2%)
    all_gather x1, blocking collectives, local(): lax.all_gather(col_feats, 'blk', axis=0, tiled=True)  15.4 us
    all_gather x1, blocking collectives, local(): lax.all_gather(col_vals.astype(jnp.bfloat16), 'blk', axis=0, tiled=True)  11.5 us
    psum x1, blocking collectives, local(): total = lax.psum(jnp.sum(jnp.abs(block_averaged)), 'blk')  8.97 us
    all_gather x1, blocking collectives, local(): block_feats = lax.all_gather(unit_rows, 'cols', axis=0, tiled=True)  5.62 us
    psum x1, blocking collectives, local(): lax.psum(lax.psum((partial_sums[0], partial_sums[1]), 'sub'), 'cols')  4.91 us
    psum x1, blocking collectives, local(): lax.psum((partial_sums[0], partial_sums[1]), 'sub')  2.45 us
    all_gather x1, blocking collectives, local(): gathered = lax.all_gather(features, 'sub', axis=1, tiled=True)  2.28 us
    div x2, other arithmetic, local(): return (averaged / mean_abs, degree / points)  1.28 us

profile of v1, /device:TPU:0, one launch (start us, length us, event | category | flops | bytes accessed | tf_op | source)
XLA Modules:
  0.0 55.6 jit_solution(12246513549719111006)
XLA Ops:
  0.6 0.0 copy-start
  0.7 2.3 %all_gather.12 = bf16[256,256]{1,0:T(8,128)(2,1)S(1)} all-gather(bf16[256,128]{1,0:T(8,128)(2,1)} %param.2), channel_id=1, replica_groups=mesh['groups'=2,'blk'=4,'cols'=2,'sub'=2] {'sub'}, dimensions={1}, use_global_device_ids=true | all-gather | bytes 196608 | tf_op jit(solution)/shard_map/all_gather | solution.py:48
  2.9 0.1 fusion.5
  3.1 0.1 fusion.7
  3.2 15.4 %all_gather.14 = bf16[512,256]{1,0:T(8,128)(2,1)S(1)} all-gather(bf16[128,256]{1,0:T(8,128)(2,1)S(1)} %constant_dynamic-slice_fusion), channel_id=1, replica_groups=mesh['groups'=2,'blk'=4,'cols'=2,'sub'=2] {'blk'}, dimensions={0}, use_global_device_ids=true | all-gather | bytes 327680 | tf_op jit(solution)/shard_map/all_gather | solution.py:64
  18.6 5.6 %all_gather.13 = bf16[512,256]{1,0:T(8,128)(2,1)S(1)} all-gather(bf16[256,256]{1,0:T(8,128)(2,1)S(1)} %fusion.7), channel_id=1, replica_groups=mesh['groups'=2,'blk'=4,'cols'=2,'sub'=2] {'cols'}, dimensions={0}, use_global_device_ids=true | all-gather | bytes 393216 | tf_op jit(solution)/shard_map/all_gather | solution.py:59
  24.2 0.4 fusion.10
  24.6 0.0 copy-done
  24.6 0.1 convert_bitcast_fusion
  24.7 11.5 %all-gather = bf16[4,1,128]{2,1,0:T(2,128)(2,1)S(1)} all-gather(bf16[1,1,128]{2,1,0:T(2,128)(2,1)S(1)} %convert_bitcast_fusion), channel_id=1, replica_groups=mesh['groups'=2,'blk'=4,'cols'=2,'sub'=2] {'blk'}, dimensions={0}, use_global_device_ids=true | all-gather | bytes 1280 | tf_op jit(solution)/shard_map/all_gather | solution.py:65
  36.2 0.4 fusion.8
  36.7 2.4 %all-reduce = (f32[512]{0:T(512)S(1)}, f32[512]{0:T(512)S(1)}) all-reduce(f32[512]{0:T(512)S(1)} %bitcast.9, f32[512]{0:T(512)S(1)} %get-tuple-element.8), channel_id=1, replica_groups=mesh['groups'=2,'blk'=4,'cols'=2,'sub'=2] {'sub'}, use_global_device_ids=true, to_apply=%region_1.0 | all-reduce | flops 1024 | bytes 8192 | tf_op jit(solution)/shard_map/psum | solution.py:71
  39.1 4.9 %all-reduce.1 = (f32[512]{0:T(512)S(1)}, f32[512]{0:T(512)S(1)}) all-reduce(f32[512]{0:T(512)S(1)} %get-tuple-element.2, f32[512]{0:T(512)S(1)} %get-tuple-element.3), channel_id=1, replica_groups=mesh['groups'=2,'blk'=4,'cols'=2,'sub'=2] {'cols'}, use_global_device_ids=true, to_apply=%region_2.0 | all-reduce | flops 1024 | bytes 8192 | tf_op jit(solution)/shard_map/psum | solution.py:70
  44.0 0.6 %dynamic-slice_multiply_fusion = f32[256]{0:T(256)} fusion(f32[512]{0:T(512)S(1)} %get-tuple-element.5, s32[]{:T(128)S(6)} %select_n.9), kind=kLoop, calls=%fused_computation.14 | loop fusion | flops 256 | bytes 2052 | tf_op jit(solution)/shard_map/div | solution.py:79
  44.7 0.6 %abs_reduce_fusion = (f32[]{:T(128)}, f32[512]{0:T(512)S(1)}) fusion(f32[512]{0:T(512)S(1)} %get-tuple-element.4, f32[512]{0:T(512)S(1)} %get-tuple-element.5), kind=kLoop, calls=%fused_computation.13 | loop fusion | flops 1535 | bytes 6148 | tf_op jit(solution)/shard_map/reduce_sum | solution.py:74
  45.3 9.0 %psum.39 = f32[]{:T(128)} all-reduce(f32[]{:T(128)} %get-tuple-element.6), channel_id=1, replica_groups=mesh['groups'=2,'blk'=4,'cols'=2,'sub'=2] {'blk'}, use_global_device_ids=true, to_apply=%region_7.0 | all-reduce | flops 1 | bytes 8 | tf_op jit(solution)/shard_map/psum | solution.py:74
  54.9 0.6 %dynamic-slice_divide_fusion = f32[256]{0:T(256)} fusion(f32[512]{0:T(512)S(1)} %get-tuple-element.7, s32[]{:T(128)S(6)} %select_n.9, f32[]{:T(128)S(6)} %add.44), kind=kLoop, calls=%fused_computation.15 | loop fusion | flops 256 | bytes 2056 | tf_op jit(solution)/shard_map/div | solution.py:79
  (2 shorter events, 0.0 us)
Async XLA Ops:
  0.6 24.0 %copy-start = (f32[256]{0:T(256)S(1)}, f32[256]{0:T(256)}, u32[]{:S(2)}) copy-start(f32[256]{0:T(256)} %param.3) | copy-start | bytes 3076
